TPU v7x, 32 devices: a whole 2x2x4 slice. The times are simulated.
32 devices in a mesh: case: 4 (over z), span: 2 (over x), vert: 4 (over y, core).
Axes of the slice: x: 2, y: 2, z: 4, core: 2. Of those that a mesh axis runs over, the one named last changes fastest.
Arguments:
- state: float32 [8, 4, 16, 32, 512], P('case', None, 'span', 'vert'), may hold values from -3 to 4.5
- turbine_x: int32 [8, 6], P('case'), may hold values from 128 to 511
- turbine_y: int32 [8, 6], P('case'), may hold values from 0 to 15
- yaw_index: int32 [8], P('case'), may hold values from 0 to 7
Outputs:
- final_state: float32 [8, 4, 16, 32, 512], P('case', None, 'span', 'vert')
All inputs are finite; a program needn't handle non-finite values.
Results may differ from a plain program's by a relative error of at most 0.0003.
Values sent between devices are 32-bit elements; how exact they have to be, the bound alone decides.
No kernel may reach another device: no remote copies, remote signals or barrier semaphores. Data moves between devices by JAX's collectives and lax.ppermute only.
A program may use at most 64 MiB of HBM per device.

v0:
```python
import jax
import jax.numpy as jnp
from jax import lax
from jax.sharding import PartitionSpec as P

X = 512
STEPS = 3
DISK = 8


U_MEAN = 1.0
VISC = 0.04
THRUST = 0.75
TIME_STEP = 0.1
YAW_STEP = 0.15


def extended_2(shard, sides, width):
    for axis, dim in sides:
        size, length = (lax.axis_size(axis), shard.shape[dim])
        up = [(i, (i + 1) % size) for i in range(size)]
        down = [(j, i) for i, j in up]
        last = lax.slice_in_dim(shard, length - width, length, axis=dim)
        leading = lax.slice_in_dim(shard, 0, width, axis=dim)
        before = lax.ppermute(last, axis, up)
        after = lax.ppermute(leading, axis, down)
        shard = jnp.concatenate([before, shard, after], axis=dim)
    return shard


def entering(part, axis, combine, identity):
    place = lax.axis_index(axis)
    gathered = jax.tree.map(lambda a: lax.all_gather(a, axis), part)
    state = jax.tree.map(lambda a, e: jnp.zeros_like(a) + jnp.asarray(e, a.dtype), part, identity)

    def one(step, state):
        return combine(
            state, jax.tree.map(lambda a: lax.dynamic_index_in_dim(a, step, 0, False), gathered)
        )

    return lax.fori_loop(0, place, one, state)


def tendency(center, east, west, north, south, upper, lower, weight, cos_yaw, sin_yaw):
    grad_x = (east - west) * 0.5
    grad_y = (north - south) * 0.5
    grad_z = (upper - lower) * 0.5
    laplace = east + west + north + south + upper + lower - 6.0 * center
    vel_u = center[..., 1, :, :, :]
    vel_v = center[..., 2, :, :, :]
    vel_w = center[..., 3, :, :, :]
    dux = grad_x[..., 1, :, :, :]
    dvy = grad_y[..., 2, :, :, :]
    dwz = grad_z[..., 3, :, :, :]
    duy = grad_y[..., 1, :, :, :]
    duz = grad_z[..., 1, :, :, :]
    strain = dux * dux + dvy * dvy + dwz * dwz + duy * duy + duz * duz
    viscous = VISC * jnp.sqrt(1.0 + strain)
    speed = U_MEAN + vel_u
    flow = -(
        jnp.expand_dims(speed, -4) * grad_x
        + jnp.expand_dims(vel_v, -4) * grad_y
        + jnp.expand_dims(vel_w, -4) * grad_z
    )
    flow = flow + jnp.expand_dims(viscous, -4) * laplace
    normal = speed * cos_yaw + vel_v * sin_yaw
    thrust = THRUST * normal * jnp.abs(normal) * weight
    extra = jnp.stack(
        [
            -(dux + dvy + dwz),
            -grad_x[..., 0, :, :, :] - thrust * cos_yaw,
            -grad_y[..., 0, :, :, :] - thrust * sin_yaw,
            -grad_z[..., 0, :, :, :],
        ],
        axis=-4,
    )
    return flow + extra


def extended(fields):
    padded = extended_2(fields, (("span", 2), ("vert", 3)), 1)
    vert_at = lax.axis_index("vert")
    bottom = jnp.where(vert_at == 0, 0.0, padded[:, :, :, :1, :])
    summit = jnp.where(vert_at == lax.axis_size("vert") - 1, 0.0, padded[:, :, :, -1:, :])
    padded = jnp.concatenate([bottom, padded[:, :, :, 1:-1, :], summit], axis=3)
    return padded


def stencil(fields, padded, weight, cos_yaw, sin_yaw):
    east = jnp.roll(fields, -1, axis=4)
    west = jnp.roll(fields, 1, axis=4)
    north = padded[:, :, 2:, 1:-1, :]
    south = padded[:, :, :-2, 1:-1, :]
    upper = padded[:, :, 1:-1, 2:, :]
    lower = padded[:, :, 1:-1, :-2, :]
    return tendency(fields, east, west, north, south, upper, lower, weight, cos_yaw, sin_yaw)


def rate(fields, weight, cos_yaw, sin_yaw):
    return stencil(fields, extended(fields), weight, cos_yaw, sin_yaw)


def make_weight(turbine_x, turbine_y, along_y, along_z, total_y, total_z, active):
    along_x = jnp.arange(X, dtype=jnp.int32)
    hit_x = (along_x[None, None, :] == turbine_x[:, :, None]).astype(jnp.float32)
    hit_y = ((along_y[None, None, :] - turbine_y[:, :, None]) % total_y < DISK).astype(jnp.float32)
    plane = jnp.einsum("dky,dkx->dyx", hit_y, hit_x, precision=lax.Precision.HIGHEST)
    lower_half = (along_z < total_z // 2).astype(jnp.float32)
    return plane[:, :, None, :] * lower_half[None, None, :, None] * active[:, None, None, None]


def first_held(earlier, later):
    keep = earlier[1] > 0.0
    return (jnp.where(keep, earlier[0], later[0]), jnp.maximum(earlier[1], later[1]))


def body(state, turbine_x, turbine_y, yaw_index):
    slots = state.shape[0]
    rows_y = state.shape[2]
    rows_z = state.shape[3]
    total_y = rows_y * lax.axis_size("span")
    total_z = rows_z * lax.axis_size("vert")
    domain = lax.axis_index("case") * slots + jnp.arange(slots, dtype=jnp.int32)
    active = (domain > 0).astype(jnp.float32)
    along_y = lax.axis_index("span") * rows_y + jnp.arange(rows_y, dtype=jnp.int32)
    along_z = lax.axis_index("vert") * rows_z + jnp.arange(rows_z, dtype=jnp.int32)
    weight = make_weight(turbine_x, turbine_y, along_y, along_z, total_y, total_z, active)
    angle = (yaw_index.astype(jnp.float32) - 3.5) * YAW_STEP
    cos_yaw = jnp.cos(angle)[:, None, None, None]
    sin_yaw = jnp.sin(angle)[:, None, None, None]
    width = X // 4
    ramp = 0.5 * (1.0 - jnp.cos(jnp.pi * (jnp.arange(width, dtype=jnp.float32) + 1.0) / width))
    case_at = lax.axis_index("case")
    for step in range(STEPS):
        first = rate(state, weight, cos_yaw, sin_yaw)
        middle = state + TIME_STEP * first
        second = rate(middle, weight, cos_yaw, sin_yaw)
        state = state + 0.5 * TIME_STEP * (first + second)
        front = state[..., :width]
        own_fringe = front[0]
        marker = jnp.ones((), jnp.float32)
        blank = (jnp.zeros_like(own_fringe), jnp.zeros((), jnp.float32))
        passed = entering((own_fringe, marker), "case", first_held, blank)
        source = jnp.where(case_at == 0, own_fringe, passed[0])
        front = front + ramp * (source[None] - front)
        state = jnp.concatenate([front, state[..., width:]], axis=4)
    return state


def solution(mesh):
    return jax.shard_map(
        body,
        mesh=mesh,
        in_specs=(
            P("case", None, "span", "vert", None),
            P("case", None),
            P("case", None),
            P("case"),
        ),
        out_specs=P("case", None, "span", "vert", None),
        check_vma=False,
    )
```

profile of v0, /device:TPU:28, one launch (start us, length us, event | category | flops | bytes accessed | tf_op | source)
XLA Modules:
  0.0 179.2 jit_solution(10884693415448655372)
XLA Ops:
  3.7 2.0 %fusion.137 = (f32[2,4,8,8,511]{4,3,2,1,0:T(8,128)S(1)}, f32[2,4,8,8,511]{4,3,2,1,0:T(8,128)S(1)}) fusion(f32[2,4,8,8,512]{4,3,2,1,0:T(8,128)} %param.10), kind=kLoop, calls=%fused_computation.359 | loop fusion | bytes 4186112 | tf_op jit(solution)/shard_map/jit(_roll_static)/slice | solution.py:90
  10.3 2.1 %fusion.14 = (f32[2,4,8,8,512]{4,3,2,1,0:T(8,128)}, f32[2,4,10,8,512]{4,3,2,1,0:T(8,128)S(1)}) fusion(f32[2,4,1,8,512]{4,3,2,1,0:T(8,128)} %collective-permute-done, f32[2,4,8,8,512]{4,3,2,1,0:T(8,128)S(1)} %copy-done, f32[2,4,1,8,512]{4,3,2,1,0:T(8,128)} %collective-permute-done.1, f32[2,4,10,8,512]{4,3,2,1,0:T(8,128)S(1)} %constant_dynamic-update-slice_fusion.2), kind=kLoop, calls=%fused_computation.121 | loop fusion | flops 1048576 | bytes 3407872 | tf_op jit(solution)/shard_map/mul | solution.py:46
  15.4 8.1 %all-reduce = f32[4]{0:T(128)S(1)} all-reduce(f32[4]{0:T(128)S(1)} %dynamic-update-slice), channel_id=1, replica_groups=mesh['case'=4,'span'=2,'vert'=4] {'case'}, use_global_device_ids=true, to_apply=%add | all-reduce | flops 4 | bytes 32
  26.2 3.6 %collective-permute-done.3 = f32[2,4,10,1,512]{4,3,2,1,0:T(1,128)S(1)} collective-permute-done((f32[2,4,10,1,512]{4,3,2,1,0:T(1,128)S(1)}, f32[2,4,10,1,512]{4,3,2,1,0:T(1,128)S(1)}, u32[]{:S(2)}, u32[]{:S(2)}) %collective-permute-start.3) | collective-permute-done | bytes 163872 | tf_op jit(solution)/shard_map/ppermute | solution.py:25
  32.4 2.4 %multiply_add_fusion.2 = (f32[2,4,8,8,512]{4,3,2,1,0:T(8,128)S(1)}, f32[2,4,8,8,512]{4,3,2,1,0:T(8,128)S(1)}) fusion(f32[2,4,8,8,512]{4,3,2,1,0:T(8,128)S(1)} %copy-done, f32[2,1,8,8,512]{4,3,2,1,0:T(8,128)S(1)} %slice_negate_fusion.15, f32[2,1,8,8,512]{4,3,2,1,0:T(8,128)S(1)} %get-tuple-element.200, f32[2,1,8,8,512]{4,3,2,1,0:T(8,128)S(1)} %get-tuple-element.199, ...), kind=kLoop, calls=%fused_computation.119 | loop fusion | flops 7864320 | bytes 9240576 | tf_op jit(solution)/shard_map/add | solution.py:136
  37.3 3.2 %collective-permute-done.4 = f32[2,4,1,8,512]{4,3,2,1,0:T(8,128)S(1)} collective-permute-done((f32[2,4,1,8,512]{4,3,2,1,0:T(8,128)S(1)}, f32[2,4,1,8,512]{4,3,2,1,0:T(8,128)S(1)}, u32[]{:S(2)}, u32[]{:S(2)}) %collective-permute-start.4) | collective-permute-done | bytes 131104 | tf_op jit(solution)/shard_map/ppermute | solution.py:26
  43.3 2.3 %collective-permute-done.6 = f32[2,4,10,1,512]{4,3,2,1,0:T(1,128)S(1)} collective-permute-done((f32[2,4,10,1,512]{4,3,2,1,0:T(1,128)S(1)}, f32[2,4,10,1,512]{4,3,2,1,0:T(1,128)S(1)}, u32[]{:S(2)}, u32[]{:S(2)}) %collective-permute-start.6) | collective-permute-done | bytes 163872 | tf_op jit(solution)/shard_map/ppermute | solution.py:26
  45.7 2.7 %collective-permute-done.7 = f32[2,4,10,1,512]{4,3,2,1,0:T(1,128)S(1)} collective-permute-done((f32[2,4,10,1,512]{4,3,2,1,0:T(1,128)S(1)}, f32[2,4,10,1,512]{4,3,2,1,0:T(1,128)S(1)}, u32[]{:S(2)}, u32[]{:S(2)}) %collective-permute-start.7) | collective-permute-done | bytes 163872 | tf_op jit(solution)/shard_map/ppermute | solution.py:25
  51.3 16.0 %all_gather.14 = f32[4,4,8,8,128]{4,3,2,1,0:T(8,128)S(1)} all-gather(f32[1,4,8,8,128]{4,3,2,1,0:T(8,128)S(1)} %slice.653), channel_id=1, replica_groups=mesh['case'=4,'span'=2,'vert'=4] {'case'}, dimensions={0}, use_global_device_ids=true | all-gather | bytes 655360 | tf_op jit(solution)/shard_map/all_gather | solution.py:33
  67.3 3.9 %while.36 = (s32[]{:T(128)}, f32[4,8,8,128]{3,2,1,0:T(8,128)S(1)}, f32[]{:T(128)}, s32[]{:T(128)}, f32[4,4,8,8,128]{4,3,2,1,0:T(8,128)S(1)}, /*index=5*/f32[4]{0...) while((s32[]{:T(128)}, f32[4,8,8,128]{3,2,1,0:T(8,128)S(1)}, f32[]{:T(128)}, s32[]{:T(128)}, ...), condition=%wide.region_1.2_spmd, body=%wide.region_0.1_spmd.sunk | while | flops 32775 | bytes 393389 | solution.py:41
  74.3 2.5 %collective-permute-done.8 = f32[2,4,1,8,512]{4,3,2,1,0:T(8,128)S(1)} collective-permute-done((f32[2,4,1,8,512]{4,3,2,1,0:T(8,128)S(1)}, f32[2,4,1,8,512]{4,3,2,1,0:T(8,128)S(1)}, u32[]{:S(2)}, u32[]{:S(2)}) %collective-permute-start.8) | collective-permute-done | bytes 131104 | tf_op jit(solution)/shard_map/ppermute | solution.py:26
  79.5 3.1 %collective-permute-done.10 = f32[2,4,10,1,512]{4,3,2,1,0:T(1,128)S(1)} collective-permute-done((f32[2,4,10,1,512]{4,3,2,1,0:T(1,128)S(1)}, f32[2,4,10,1,512]{4,3,2,1,0:T(1,128)S(1)}, u32[]{:S(2)}, u32[]{:S(2)}) %collective-permute-start.10) | collective-permute-done | bytes 163872 | tf_op jit(solution)/shard_map/ppermute | solution.py:26
  89.3 3.7 %collective-permute-done.12 = f32[2,4,1,8,512]{4,3,2,1,0:T(8,128)S(1)} collective-permute-done((f32[2,4,1,8,512]{4,3,2,1,0:T(8,128)S(1)}, f32[2,4,1,8,512]{4,3,2,1,0:T(8,128)S(1)}, u32[]{:S(2)}, u32[]{:S(2)}) %collective-permute-start.12) | collective-permute-done | bytes 131104 | tf_op jit(solution)/shard_map/ppermute | solution.py:26
  96.0 2.4 %collective-permute-done.14 = f32[2,4,10,1,512]{4,3,2,1,0:T(1,128)S(1)} collective-permute-done((f32[2,4,10,1,512]{4,3,2,1,0:T(1,128)S(1)}, f32[2,4,10,1,512]{4,3,2,1,0:T(1,128)S(1)}, u32[]{:S(2)}, u32[]{:S(2)}) %collective-permute-start.14) | collective-permute-done | bytes 163872 | tf_op jit(solution)/shard_map/ppermute | solution.py:26
  98.6 3.3 %collective-permute-done.15 = f32[2,4,10,1,512]{4,3,2,1,0:T(1,128)S(1)} collective-permute-done((f32[2,4,10,1,512]{4,3,2,1,0:T(1,128)S(1)}, f32[2,4,10,1,512]{4,3,2,1,0:T(1,128)S(1)}, u32[]{:S(2)}, u32[]{:S(2)}) %collective-permute-start.15) | collective-permute-done | bytes 163872 | tf_op jit(solution)/shard_map/ppermute | solution.py:25
  104.8 16.0 %all_gather.16 = f32[4,4,8,8,128]{4,3,2,1,0:T(8,128)S(1)} all-gather(f32[1,4,8,8,128]{4,3,2,1,0:T(8,128)S(1)} %slice.697), channel_id=1, replica_groups=mesh['case'=4,'span'=2,'vert'=4] {'case'}, dimensions={0}, use_global_device_ids=true | all-gather | bytes 655360 | tf_op jit(solution)/shard_map/all_gather | solution.py:33
  120.8 3.9 %while.37 = (s32[]{:T(128)}, f32[4,8,8,128]{3,2,1,0:T(8,128)S(1)}, f32[]{:T(128)}, s32[]{:T(128)}, f32[4,4,8,8,128]{4,3,2,1,0:T(8,128)S(1)}, /*index=5*/f32[4]{0...) while((s32[]{:T(128)}, f32[4,8,8,128]{3,2,1,0:T(8,128)S(1)}, f32[]{:T(128)}, s32[]{:T(128)}, ...), condition=%wide.region_3.4_spmd, body=%wide.region_2.3_spmd.sunk | while | flops 32775 | bytes 393389 | solution.py:41
  127.8 2.5 %collective-permute-done.16 = f32[2,4,1,8,512]{4,3,2,1,0:T(8,128)S(1)} collective-permute-done((f32[2,4,1,8,512]{4,3,2,1,0:T(8,128)S(1)}, f32[2,4,1,8,512]{4,3,2,1,0:T(8,128)S(1)}, u32[]{:S(2)}, u32[]{:S(2)}) %collective-permute-start.16) | collective-permute-done | bytes 131104 | tf_op jit(solution)/shard_map/ppermute | solution.py:26
  132.7 3.2 %collective-permute-done.18 = f32[2,4,10,1,512]{4,3,2,1,0:T(1,128)S(1)} collective-permute-done((f32[2,4,10,1,512]{4,3,2,1,0:T(1,128)S(1)}, f32[2,4,10,1,512]{4,3,2,1,0:T(1,128)S(1)}, u32[]{:S(2)}, u32[]{:S(2)}) %collective-permute-start.18) | collective-permute-done | bytes 163872 | tf_op jit(solution)/shard_map/ppermute | solution.py:26
  136.1 1.7 collective-permute-done.19
  142.9 4.1 %collective-permute-done.20 = f32[2,4,1,8,512]{4,3,2,1,0:T(8,128)S(1)} collective-permute-done((f32[2,4,1,8,512]{4,3,2,1,0:T(8,128)S(1)}, f32[2,4,1,8,512]{4,3,2,1,0:T(8,128)S(1)}, u32[]{:S(2)}, u32[]{:S(2)}) %collective-permute-start.20) | collective-permute-done | bytes 131104 | tf_op jit(solution)/shard_map/ppermute | solution.py:26
  151.6 3.5 %collective-permute-done.23 = f32[2,4,10,1,512]{4,3,2,1,0:T(1,128)S(1)} collective-permute-done((f32[2,4,10,1,512]{4,3,2,1,0:T(1,128)S(1)}, f32[2,4,10,1,512]{4,3,2,1,0:T(1,128)S(1)}, u32[]{:S(2)}, u32[]{:S(2)}) %collective-permute-start.23) | collective-permute-done | bytes 163872 | tf_op jit(solution)/shard_map/ppermute | solution.py:25
  157.9 16.1 %all_gather.17 = f32[4,4,8,8,128]{4,3,2,1,0:T(8,128)S(1)} all-gather(f32[1,4,8,8,128]{4,3,2,1,0:T(8,128)S(1)} %slice.741), channel_id=1, replica_groups=mesh['case'=4,'span'=2,'vert'=4] {'case'}, dimensions={0}, use_global_device_ids=true | all-gather | bytes 655360 | tf_op jit(solution)/shard_map/all_gather | solution.py:33
  174.1 3.9 %while.38 = (s32[]{:T(128)}, f32[4,8,8,128]{3,2,1,0:T(8,128)S(1)}, f32[]{:T(128)}, s32[]{:T(128)}, f32[4,4,8,8,128]{4,3,2,1,0:T(8,128)S(1)}, /*index=5*/f32[4]{0...) while((s32[]{:T(128)}, f32[4,8,8,128]{3,2,1,0:T(8,128)S(1)}, f32[]{:T(128)}, s32[]{:T(128)}, ...), condition=%wide.region_5.6_spmd, body=%wide.region_4.5_spmd.sunk | while | flops 32775 | bytes 393389 | solution.py:41
  (173 shorter events, 67.5 us)
Async XLA Ops:
  1.7 7.7 %collective-permute-start.1 = (f32[2,4,1,8,512]{4,3,2,1,0:T(8,128)}, f32[2,4,1,8,512]{4,3,2,1,0:T(8,128)}, u32[]{:S(2)}, u32[]{:S(2)}) collective-permute-start(f32[2,4,1,8,512]{4,3,2,1,0:T(8,128)} %get-tuple-element.262), channel_id=1, source_target_pairs={{0,4},{4,0},{1,5},{5,1},{2,6},{6,2},{3,7},{7,3},{8,12},{12,8},{9,1... | collective-permute-start | bytes 393224 | tf_op jit(solution)/shard_map/ppermute | solution.py:25
  3.2 7.2 %collective-permute-start = (f32[2,4,1,8,512]{4,3,2,1,0:T(8,128)}, f32[2,4,1,8,512]{4,3,2,1,0:T(8,128)}, u32[]{:S(2)}, u32[]{:S(2)}) collective-permute-start(f32[2,4,1,8,512]{4,3,2,1,0:T(8,128)} %get-tuple-element.261), channel_id=1, source_target_pairs={{4,0},{0,4},{5,1},{1,5},{6,2},{2,6},{7,3},{3,7},{12,8},{8,12},{13,... | collective-permute-start | bytes 393224 | tf_op jit(solution)/shard_map/ppermute | solution.py:26
  15.4 9.7 %collective-permute-start.2 = (f32[2,4,10,1,512]{4,3,2,1,0:T(1,128)}, f32[2,4,10,1,512]{4,3,2,1,0:T(1,128)}, u32[]{:S(2)}, u32[]{:S(2)}) collective-permute-start(f32[2,4,10,1,512]{4,3,2,1,0:T(1,128)} %get-tuple-element.186), channel_id=1, source_target_pairs={{1,0},{2,1},{3,2},{0,3},{5,4},{6,5},{7,6},{4,7},{9,8},{10,9},{11,1... | collective-permute-start | bytes 491528 | tf_op jit(solution)/shard_map/ppermute | solution.py:26
  25.0 4.8 %collective-permute-start.3 = (f32[2,4,10,1,512]{4,3,2,1,0:T(1,128)S(1)}, f32[2,4,10,1,512]{4,3,2,1,0:T(1,128)S(1)}, u32[]{:S(2)}, u32[]{:S(2)}) collective-permute-start(f32[2,4,10,1,512]{4,3,2,1,0:T(1,128)S(1)} %copy-done.8), channel_id=1, source_target_pairs={{0,1},{1,2},{2,3},{3,0},{4,5},{5,6},{6,7},{7,4},{8,9},{9,10},{10,1... | collective-permute-start | bytes 491528 | tf_op jit(solution)/shard_map/ppermute | solution.py:25
  35.1 5.4 %collective-permute-start.4 = (f32[2,4,1,8,512]{4,3,2,1,0:T(8,128)S(1)}, f32[2,4,1,8,512]{4,3,2,1,0:T(8,128)S(1)}, u32[]{:S(2)}, u32[]{:S(2)}) collective-permute-start(f32[2,4,1,8,512]{4,3,2,1,0:T(8,128)S(1)} %get-tuple-element.251), channel_id=1, source_target_pairs={{4,0},{0,4},{5,1},{1,5},{6,2},{2,6},{7,3},{3,7},{12,8},{8,12},{13,... | collective-permute-start | bytes 393224 | tf_op jit(solution)/shard_map/ppermute | solution.py:26
  36.7 5.2 %collective-permute-start.5 = (f32[2,4,1,8,512]{4,3,2,1,0:T(8,128)S(1)}, f32[2,4,1,8,512]{4,3,2,1,0:T(8,128)S(1)}, u32[]{:S(2)}, u32[]{:S(2)}) collective-permute-start(f32[2,4,1,8,512]{4,3,2,1,0:T(8,128)S(1)} %get-tuple-element.250), channel_id=1, source_target_pairs={{0,4},{4,0},{1,5},{5,1},{2,6},{6,2},{3,7},{7,3},{8,12},{12,8},{9,1... | collective-permute-start | bytes 393224 | tf_op jit(solution)/shard_map/ppermute | solution.py:25
  42.1 3.4 %collective-permute-start.6 = (f32[2,4,10,1,512]{4,3,2,1,0:T(1,128)S(1)}, f32[2,4,10,1,512]{4,3,2,1,0:T(1,128)S(1)}, u32[]{:S(2)}, u32[]{:S(2)}) collective-permute-start(f32[2,4,10,1,512]{4,3,2,1,0:T(1,128)S(1)} %get-tuple-element.184), channel_id=1, source_target_pairs={{1,0},{2,1},{3,2},{0,3},{5,4},{6,5},{7,6},{4,7},{9,8},{10,9},{11,1... | collective-permute-start | bytes 491528 | tf_op jit(solution)/shard_map/ppermute | solution.py:26
  42.8 5.6 %collective-permute-start.7 = (f32[2,4,10,1,512]{4,3,2,1,0:T(1,128)S(1)}, f32[2,4,10,1,512]{4,3,2,1,0:T(1,128)S(1)}, u32[]{:S(2)}, u32[]{:S(2)}) collective-permute-start(f32[2,4,10,1,512]{4,3,2,1,0:T(1,128)S(1)} %get-tuple-element.183), channel_id=1, source_target_pairs={{0,1},{1,2},{2,3},{3,0},{4,5},{5,6},{6,7},{7,4},{8,9},{9,10},{10,1... | collective-permute-start | bytes 491528 | tf_op jit(solution)/shard_map/ppermute | solution.py:25
  71.8 5.0 %collective-permute-start.8 = (f32[2,4,1,8,512]{4,3,2,1,0:T(8,128)S(1)}, f32[2,4,1,8,512]{4,3,2,1,0:T(8,128)S(1)}, u32[]{:S(2)}, u32[]{:S(2)}) collective-permute-start(f32[2,4,1,8,512]{4,3,2,1,0:T(8,128)S(1)} %get-tuple-element.242), channel_id=1, source_target_pairs={{4,0},{0,4},{5,1},{1,5},{6,2},{2,6},{7,3},{3,7},{12,8},{8,12},{13,... | collective-permute-start | bytes 393224 | tf_op jit(solution)/shard_map/ppermute | solution.py:26
  73.3 5.0 %collective-permute-start.9 = (f32[2,4,1,8,512]{4,3,2,1,0:T(8,128)S(1)}, f32[2,4,1,8,512]{4,3,2,1,0:T(8,128)S(1)}, u32[]{:S(2)}, u32[]{:S(2)}) collective-permute-start(f32[2,4,1,8,512]{4,3,2,1,0:T(8,128)S(1)} %get-tuple-element.241), channel_id=1, source_target_pairs={{0,4},{4,0},{1,5},{5,1},{2,6},{6,2},{3,7},{7,3},{8,12},{12,8},{9,1... | collective-permute-start | bytes 393224 | tf_op jit(solution)/shard_map/ppermute | solution.py:25
  78.5 4.2 %collective-permute-start.10 = (f32[2,4,10,1,512]{4,3,2,1,0:T(1,128)S(1)}, f32[2,4,10,1,512]{4,3,2,1,0:T(1,128)S(1)}, u32[]{:S(2)}, u32[]{:S(2)}) collective-permute-start(f32[2,4,10,1,512]{4,3,2,1,0:T(1,128)S(1)} %get-tuple-element.180), channel_id=1, source_target_pairs={{1,0},{2,1},{3,2},{0,3},{5,4},{6,5},{7,6},{4,7},{9,8},{10,9},{11,1... | collective-permute-start | bytes 491528 | tf_op jit(solution)/shard_map/ppermute | solution.py:26
  78.8 5.4 %collective-permute-start.11 = (f32[2,4,10,1,512]{4,3,2,1,0:T(1,128)S(1)}, f32[2,4,10,1,512]{4,3,2,1,0:T(1,128)S(1)}, u32[]{:S(2)}, u32[]{:S(2)}) collective-permute-start(f32[2,4,10,1,512]{4,3,2,1,0:T(1,128)S(1)} %get-tuple-element.179), channel_id=1, source_target_pairs={{0,1},{1,2},{2,3},{3,0},{4,5},{5,6},{6,7},{7,4},{8,9},{9,10},{10,1... | collective-permute-start | bytes 491528 | tf_op jit(solution)/shard_map/ppermute | solution.py:25
  87.1 6.0 %collective-permute-start.12 = (f32[2,4,1,8,512]{4,3,2,1,0:T(8,128)S(1)}, f32[2,4,1,8,512]{4,3,2,1,0:T(8,128)S(1)}, u32[]{:S(2)}, u32[]{:S(2)}) collective-permute-start(f32[2,4,1,8,512]{4,3,2,1,0:T(8,128)S(1)} %get-tuple-element.231), channel_id=1, source_target_pairs={{4,0},{0,4},{5,1},{1,5},{6,2},{2,6},{7,3},{3,7},{12,8},{8,12},{13,... | collective-permute-start | bytes 393224 | tf_op jit(solution)/shard_map/ppermute | solution.py:26
  88.5 5.9 %collective-permute-start.13 = (f32[2,4,1,8,512]{4,3,2,1,0:T(8,128)S(1)}, f32[2,4,1,8,512]{4,3,2,1,0:T(8,128)S(1)}, u32[]{:S(2)}, u32[]{:S(2)}) collective-permute-start(f32[2,4,1,8,512]{4,3,2,1,0:T(8,128)S(1)} %get-tuple-element.230), channel_id=1, source_target_pairs={{0,4},{4,0},{1,5},{5,1},{2,6},{6,2},{3,7},{7,3},{8,12},{12,8},{9,1... | collective-permute-start | bytes 393224 | tf_op jit(solution)/shard_map/ppermute | solution.py:25
  94.6 3.8 %collective-permute-start.14 = (f32[2,4,10,1,512]{4,3,2,1,0:T(1,128)S(1)}, f32[2,4,10,1,512]{4,3,2,1,0:T(1,128)S(1)}, u32[]{:S(2)}, u32[]{:S(2)}) collective-permute-start(f32[2,4,10,1,512]{4,3,2,1,0:T(1,128)S(1)} %get-tuple-element.176), channel_id=1, source_target_pairs={{1,0},{2,1},{3,2},{0,3},{5,4},{6,5},{7,6},{4,7},{9,8},{10,9},{11,1... | collective-permute-start | bytes 491528 | tf_op jit(solution)/shard_map/ppermute | solution.py:26
  95.9 5.9 %collective-permute-start.15 = (f32[2,4,10,1,512]{4,3,2,1,0:T(1,128)S(1)}, f32[2,4,10,1,512]{4,3,2,1,0:T(1,128)S(1)}, u32[]{:S(2)}, u32[]{:S(2)}) collective-permute-start(f32[2,4,10,1,512]{4,3,2,1,0:T(1,128)S(1)} %get-tuple-element.175), channel_id=1, source_target_pairs={{0,1},{1,2},{2,3},{3,0},{4,5},{5,6},{6,7},{7,4},{8,9},{9,10},{10,1... | collective-permute-start | bytes 491528 | tf_op jit(solution)/shard_map/ppermute | solution.py:25
  125.3 5.0 %collective-permute-start.16 = (f32[2,4,1,8,512]{4,3,2,1,0:T(8,128)S(1)}, f32[2,4,1,8,512]{4,3,2,1,0:T(8,128)S(1)}, u32[]{:S(2)}, u32[]{:S(2)}) collective-permute-start(f32[2,4,1,8,512]{4,3,2,1,0:T(8,128)S(1)} %get-tuple-element.222), channel_id=1, source_target_pairs={{4,0},{0,4},{5,1},{1,5},{6,2},{2,6},{7,3},{3,7},{12,8},{8,12},{13,... | collective-permute-start | bytes 393224 | tf_op jit(solution)/shard_map/ppermute | solution.py:26
  126.7 5.0 %collective-permute-start.17 = (f32[2,4,1,8,512]{4,3,2,1,0:T(8,128)S(1)}, f32[2,4,1,8,512]{4,3,2,1,0:T(8,128)S(1)}, u32[]{:S(2)}, u32[]{:S(2)}) collective-permute-start(f32[2,4,1,8,512]{4,3,2,1,0:T(8,128)S(1)} %get-tuple-element.221), channel_id=1, source_target_pairs={{0,4},{4,0},{1,5},{5,1},{2,6},{6,2},{3,7},{7,3},{8,12},{12,8},{9,1... | collective-permute-start | bytes 393224 | tf_op jit(solution)/shard_map/ppermute | solution.py:25
  131.9 4.1 %collective-permute-start.18 = (f32[2,4,10,1,512]{4,3,2,1,0:T(1,128)S(1)}, f32[2,4,10,1,512]{4,3,2,1,0:T(1,128)S(1)}, u32[]{:S(2)}, u32[]{:S(2)}) collective-permute-start(f32[2,4,10,1,512]{4,3,2,1,0:T(1,128)S(1)} %get-tuple-element.172), channel_id=1, source_target_pairs={{1,0},{2,1},{3,2},{0,3},{5,4},{6,5},{7,6},{4,7},{9,8},{10,9},{11,1... | collective-permute-start | bytes 491528 | tf_op jit(solution)/shard_map/ppermute | solution.py:26
  132.2 5.7 %collective-permute-start.19 = (f32[2,4,10,1,512]{4,3,2,1,0:T(1,128)S(1)}, f32[2,4,10,1,512]{4,3,2,1,0:T(1,128)S(1)}, u32[]{:S(2)}, u32[]{:S(2)}) collective-permute-start(f32[2,4,10,1,512]{4,3,2,1,0:T(1,128)S(1)} %get-tuple-element.171), channel_id=1, source_target_pairs={{0,1},{1,2},{2,3},{3,0},{4,5},{5,6},{6,7},{7,4},{8,9},{9,10},{10,1... | collective-permute-start | bytes 491528 | tf_op jit(solution)/shard_map/ppermute | solution.py:25
  140.7 6.3 %collective-permute-start.20 = (f32[2,4,1,8,512]{4,3,2,1,0:T(8,128)S(1)}, f32[2,4,1,8,512]{4,3,2,1,0:T(8,128)S(1)}, u32[]{:S(2)}, u32[]{:S(2)}) collective-permute-start(f32[2,4,1,8,512]{4,3,2,1,0:T(8,128)S(1)} %get-tuple-element.211), channel_id=1, source_target_pairs={{4,0},{0,4},{5,1},{1,5},{6,2},{2,6},{7,3},{3,7},{12,8},{8,12},{13,... | collective-permute-start | bytes 393224 | tf_op jit(solution)/shard_map/ppermute | solution.py:26
  142.2 6.2 %collective-permute-start.21 = (f32[2,4,1,8,512]{4,3,2,1,0:T(8,128)S(1)}, f32[2,4,1,8,512]{4,3,2,1,0:T(8,128)S(1)}, u32[]{:S(2)}, u32[]{:S(2)}) collective-permute-start(f32[2,4,1,8,512]{4,3,2,1,0:T(8,128)S(1)} %get-tuple-element.210), channel_id=1, source_target_pairs={{0,4},{4,0},{1,5},{5,1},{2,6},{6,2},{3,7},{7,3},{8,12},{12,8},{9,1... | collective-permute-start | bytes 393224 | tf_op jit(solution)/shard_map/ppermute | solution.py:25
  148.6 2.9 %collective-permute-start.22 = (f32[2,4,10,1,512]{4,3,2,1,0:T(1,128)S(1)}, f32[2,4,10,1,512]{4,3,2,1,0:T(1,128)S(1)}, u32[]{:S(2)}, u32[]{:S(2)}) collective-permute-start(f32[2,4,10,1,512]{4,3,2,1,0:T(1,128)S(1)} %get-tuple-element.168), channel_id=1, source_target_pairs={{1,0},{2,1},{3,2},{0,3},{5,4},{6,5},{7,6},{4,7},{9,8},{10,9},{11,1... | collective-permute-start | bytes 491528 | tf_op jit(solution)/shard_map/ppermute | solution.py:26
  149.2 6.0 %collective-permute-start.23 = (f32[2,4,10,1,512]{4,3,2,1,0:T(1,128)S(1)}, f32[2,4,10,1,512]{4,3,2,1,0:T(1,128)S(1)}, u32[]{:S(2)}, u32[]{:S(2)}) collective-permute-start(f32[2,4,10,1,512]{4,3,2,1,0:T(1,128)S(1)} %get-tuple-element.167), channel_id=1, source_target_pairs={{0,1},{1,2},{2,3},{3,0},{4,5},{5,6},{6,7},{7,4},{8,9},{9,10},{10,1... | collective-permute-start | bytes 491528 | tf_op jit(solution)/shard_map/ppermute | solution.py:25
  (13 other events, 24.2 us)
where the time goes:
time: 180 us; the launch traced here: 179 us
  blocking collectives  56.2 us (31%)
  waiting for transfers between devices  52 us (29%)
  other arithmetic  28.8 us (16%)
  local copies, waits for them, and re-layouts  19 us (11%)
  starting transfers between devices  16.2 us (9%)
  loops' own time  6.2 us (3%)
    all_gather x3, blocking collectives, entering(): gathered = jax.tree.map(lambda a: lax.all_gather(a, axis), part)  48.1 us
    ppermute x12, waiting for transfers between devices, extended_2(): after = lax.ppermute(leading, axis, down)  28.6 us
    ppermute x12, waiting for transfers between devices, extended_2(): before = lax.ppermute(last, axis, up)  23.4 us
    ppermute x12, starting transfers between devices, extended_2(): after = lax.ppermute(leading, axis, down)  9.04 us
    unnamed x1, blocking collectives  8.11 us
    ppermute x12, starting transfers between devices, extended_2(): before = lax.ppermute(last, axis, up)  7.13 us
    another operation x3, loops' own time, entering(): return lax.fori_loop(0, place, one, state)  6.2 us
    add x3, other arithmetic, body(): middle = state + TIME_STEP * first  5.42 us
  transfers between devices with their start and end apart: 24, of which 21 were waited for; matrix products, arithmetic and copies ran while one was open for 7% of the time, Pallas kernels for 0%

commit v1 on v0

--- a/solution.py
+++ b/solution.py
@@ -1,18 +1,354 @@
+import functools
+
 import jax
 import jax.numpy as jnp
 from jax import lax
+from jax.experimental import pallas as pl
+from jax.experimental.pallas import tpu as pltpu
 from jax.sharding import PartitionSpec as P
 
-X = 512
 STEPS = 3
 DISK = 8
-
+LANES = 128
+HALO = 2 * STEPS
 
 U_MEAN = 1.0
 VISC = 0.04
 THRUST = 0.75
 TIME_STEP = 0.1
 YAW_STEP = 0.15
+
+ROW0 = 8
+STRIP = 16
+
+
+def flat(block):
+    f, y, z, x = block.shape
+    t = x // LANES
+    return block.reshape(f, y, z, t, LANES).transpose(0, 1, 3, 2, 4).reshape(f * y * t * z, LANES)
+
+
+def unflat(rows, f, y, z, x):
+    t = x // LANES
+    lead = rows.shape[:-2]
+    n = len(lead)
+    a = rows.reshape(*lead, f, y, t, z, LANES)
+    a = jnp.swapaxes(a, n + 2, n + 3)
+    return a.reshape(*lead, f, y, z, x)
+
+
+def pack_kernel(dims, src_ref, out_ref):
+    fields, ry, rz, tiles = dims
+    lane = lax.broadcasted_iota(jnp.int32, (rz, LANES), 1)
+    for f in range(fields):
+        strip = jnp.zeros((rz, LANES), jnp.float32)
+        for y in range(ry):
+            row = (f * ry + y) * tiles * rz
+            out_ref[pl.ds((f * (ry + 1) + y) * rz, rz), :] = src_ref[pl.ds(row, rz), :]
+            after = src_ref[pl.ds(row + rz, rz), :]
+            before = src_ref[pl.ds(row + (tiles - 1) * rz, rz), :]
+            both = jnp.where(lane < LANES // 2, after, before)
+            both = pltpu.roll(both, (HALO + STRIP * y) % LANES, 1)
+            here = (lane >= STRIP * y) & (lane < STRIP * y + 2 * HALO)
+            strip = jnp.where(here, both, strip)
+        out_ref[pl.ds((f * (ry + 1) + ry) * rz, rz), :] = strip
+
+
+def main_kernel(
+    dims, ints, reals, own, got, in_own, in_got, out_own, out_got, p_own, p_in, p_out, ramp_ref,
+    mine_ref, send_ref, q, m, pq, pm, tmp, wgt,
+):
+    fields, ry, rz, tiles, nt = dims
+    ext = rz + 2 * HALO
+    total_y = 2 * ry
+    groups = total_y // 8
+    dlo, dhi, even, gate, y_off = (ints[i] for i in range(5))
+    cos_yaw, sin_yaw, active = (reals[i] for i in range(3))
+    lane = lax.broadcasted_iota(jnp.int32, (8, LANES), 1)
+    sub = lax.broadcasted_iota(jnp.int32, (8, LANES), 0)
+    first_lane = lane == 0
+    last_lane = lane == LANES - 1
+
+    def put(dst, f, t, z, group, value):
+        dst[f, t, z, pl.ds(ROW0 + 8 * group, 8), :] = value
+        if group == 0:
+            dst[f, t, z, pl.ds(ROW0 + total_y, 1), :] = value[0:1]
+        if group == groups - 1:
+            dst[f, t, z, pl.ds(ROW0 - 1, 1), :] = value[7:8]
+
+    def fill(src, half, z_src, z_dst, count):
+        def one(f, carry):
+            for t in range(tiles):
+                for k in range(count):
+                    for g in range(ry // 8):
+                        start = ((f * ry + 8 * g) * tiles + t) * rz + z_src + k
+                        value = src[pl.ds(start, 8, stride=tiles * rz), :]
+                        put(q, f, t, z_dst + k, half * (ry // 8) + g, value)
+            return carry
+
+        lax.fori_loop(0, fields, one, 0)
+
+    def fill_fringe(src, half, z_src, z_dst, count):
+        def one(f, carry):
+            base = (half * fields + f) * (ry + 1) * rz
+            strip = src[pl.ds(base + ry * rz, rz), :]
+            for y in range(ry):
+                tmp[pl.ds(y * rz, rz), :] = pltpu.roll(strip, (-(HALO + STRIP * y)) % LANES, 1)
+            for k in range(count):
+                for g in range(ry // 8):
+                    start = base + 8 * g * rz + z_src + k
+                    group = half * (ry // 8) + g
+                    put(pq, f, 0, z_dst + k, group, src[pl.ds(start, 8, stride=rz), :])
+                    value = tmp[pl.ds(8 * g * rz + z_src + k, 8, stride=rz), :]
+                    put(pq, f, 1, z_dst + k, group, value)
+            return carry
+
+        lax.fori_loop(0, fields, one, 0)
+
+    for half, src in enumerate((own, got)):
+        fill(src, half, 0, HALO, rz)
+    for half in range(2):
+        fill_fringe(p_own, half, 0, HALO, rz)
+
+    @pl.when(even == 1)
+    def _():
+        fill(out_own, 0, rz - HALO, 0, HALO)
+        fill(out_got, 1, rz - HALO, 0, HALO)
+        fill(in_own, 0, 0, HALO + rz, HALO)
+        fill(in_got, 1, 0, HALO + rz, HALO)
+        for half in range(2):
+            fill_fringe(p_out, half, rz - HALO, 0, HALO)
+            fill_fringe(p_in, half, 0, HALO + rz, HALO)
+
+    @pl.when(even == 0)
+    def _():
+        fill(in_own, 0, rz - HALO, 0, HALO)
+        fill(in_got, 1, rz - HALO, 0, HALO)
+        fill(out_own, 0, 0, HALO + rz, HALO)
+        fill(out_got, 1, 0, HALO + rz, HALO)
+        for half in range(2):
+            fill_fringe(p_in, half, rz - HALO, 0, HALO)
+            fill_fringe(p_out, half, 0, HALO + rz, HALO)
+
+    zero = jnp.zeros((ROW0 * 2 + total_y, LANES), jnp.float32)
+    for ref, width in ((m, tiles), (pm, 2), (q, tiles), (pq, 2)):
+        for z in (HALO - 1, HALO + rz):
+            outside = (z < dlo) | (z >= dhi)
+
+            def clear(ref=ref, width=width, z=z):
+                for f in range(fields):
+                    for t in range(width):
+                        ref[f, t, z] = zero
+
+            pl.when(outside)(clear)
+
+    for t in range(1, tiles):
+        for g in range(groups):
+            acc = jnp.zeros((8, LANES), jnp.float32)
+            y = y_off + 8 * g + sub
+            for k in range(nt):
+                hit = lax.rem(y - ints[5 + nt + k] + 2 * total_y, total_y) < DISK
+                hit = hit & (lane + t * LANES == ints[5 + k])
+                acc = acc + jnp.where(hit, 1.0, 0.0)
+            acc = acc * active
+            wgt[0, 0, t, g] = jnp.zeros((8, LANES), jnp.float32)
+            wgt[0, 1, t, g] = jnp.zeros((8, LANES), jnp.float32)
+            wgt[1, 0, t, g] = acc * (THRUST * cos_yaw)
+            wgt[1, 1, t, g] = acc * (THRUST * sin_yaw)
+
+    ramp = ramp_ref[...]
+
+    def stage(src, base, dst, width, k, is_domain):
+        second = k % 2 == 0
+        dt = 0.5 * TIME_STEP if second else TIME_STEP
+        half = 0.5 * dt
+        root = dt ** 0.5
+        cos_n = cos_yaw * (root / half)
+        sin_n = sin_yaw * (root / half)
+
+        def row(z, carry):
+            if is_domain:
+                on = jnp.where(z < gate, 1, 0)
+            for g in range(groups):
+                here = pl.ds(ROW0 + 8 * g, 8)
+                north_rows = pl.ds(ROW0 + 8 * g + 1, 8)
+                south_rows = pl.ds(ROW0 + 8 * g - 1, 8)
+
+                def load(t):
+                    c = [src[f, t % width, z, here, :] for f in range(fields)]
+                    left = [pltpu.roll(a, LANES - 1, 1) for a in c]
+                    right = [pltpu.roll(a, 1, 1) for a in c]
+                    return c, left, right
+
+                loaded = {}
+                for t in (-1, 0):
+                    loaded[t % width] = load(t)
+                for t in range(width):
+                    if (t + 1) % width not in loaded:
+                        loaded[(t + 1) % width] = load(t + 1)
+                    c, left, right = loaded[t]
+                    left_next = loaded[(t + 1) % width][1]
+                    right_prev = loaded[(t - 1) % width][2]
+                    east = [jnp.where(last_lane, b, a) for a, b in zip(left, left_next)]
+                    west = [jnp.where(first_lane, b, a) for a, b in zip(right, right_prev)]
+                    gx, gy, gz, lap = [], [], [], []
+                    for f in range(fields):
+                        north = src[f, t, z, north_rows, :]
+                        south = src[f, t, z, south_rows, :]
+                        upper = src[f, t, z + 1, here, :]
+                        lower = src[f, t, z - 1, here, :]
+                        gx.append(east[f] - west[f])
+                        gy.append(north - south)
+                        gz.append(upper - lower)
+                        around = ((east[f] + west[f]) + (north + south)) + (upper + lower)
+                        lap.append(around - 6.0 * c[f])
+                    speed = -half * U_MEAN - half * c[1]
+                    vel_v = -half * c[2]
+                    vel_w = -half * c[3]
+                    strain = gx[1] * gx[1] + gy[2] * gy[2] + gz[3] * gz[3]
+                    strain = strain + gy[1] * gy[1] + gz[1] * gz[1] + 4.0
+                    viscous = (0.5 * VISC * dt) * (strain * lax.rsqrt(strain))
+                    rate = [
+                        speed * gx[f] + vel_v * gy[f] + vel_w * gz[f] + viscous * lap[f]
+                        for f in range(fields)
+                    ]
+                    rate[0] = rate[0] - half * (gx[1] + gy[2] + gz[3])
+                    rate[1] = rate[1] - half * gx[0]
+                    rate[2] = rate[2] - half * gy[0]
+                    rate[3] = rate[3] - half * gz[0]
+                    if is_domain and t > 0:
+                        normal = speed * cos_n + vel_v * sin_n
+                        thrust = normal * jnp.abs(normal)
+                        rate[1] = rate[1] + thrust * wgt[on, 0, t, g]
+                        rate[2] = rate[2] + thrust * wgt[on, 1, t, g]
+                    for f in range(fields):
+                        if second:
+                            old = base[f, t, z, here, :]
+                            new = 0.5 * (old + c[f]) + rate[f]
+                            if is_domain and t == 0:
+                                new = new + ramp * (pq[f, 0, z, here, :] - new)
+                        else:
+                            new = c[f] + rate[f]
+                        if is_domain and k == HALO:
+                            out = mine_ref if g < groups // 2 else send_ref
+                            y = 8 * (g % (groups // 2))
+                            start = ((f * ry + y) * tiles + t) * rz + z - HALO
+                            out[pl.ds(start, 8, stride=tiles * rz), :] = new
+                        else:
+                            put(dst, f, t, z, g, new)
+            return carry
+
+        lax.fori_loop(jnp.maximum(k, dlo), jnp.minimum(ext - k, dhi), row, 0)
+
+    for step in range(STEPS):
+        k = 2 * step + 1
+        stage(pq, None, pm, 2, k, False)
+        stage(pm, pq, pq, 2, k + 1, False)
+        stage(q, None, m, tiles, k, True)
+        stage(m, q, q, tiles, k + 1, True)
+
+
+def join_kernel(ints, mine_ref, got_ref, out_ref):
+    out_ref[ints[0]] = mine_ref[...]
+    out_ref[1 - ints[0]] = got_ref[...]
+
+
+def swaps(size):
+    inner = [(i, i ^ 1) for i in range(size)]
+    outer = [(i, i + 1 if i % 2 else i - 1) for i in range(size)]
+    outer = [(i, j) for i, j in outer if 0 <= j < size]
+    return inner, outer
+
+
+def spread(value, axis):
+    size = lax.axis_size(axis)
+    at = lax.axis_index(axis)
+    gap = size // 2
+    while gap:
+        pairs = [(i, i + gap) for i in range(0, size, 2 * gap)]
+        moved = lax.ppermute(value, axis, pairs)
+        value = jnp.where(at % (2 * gap) == gap, moved, value)
+        gap //= 2
+    return value
+
+
+def body(state, turbine_x, turbine_y, yaw_index):
+    slots, fields, ry, rz, x = state.shape
+    tiles = x // LANES
+    nt = turbine_x.shape[1]
+    case_at, span_at, vert_at = (lax.axis_index(a) for a in ("case", "span", "vert"))
+    total_z = rz * lax.axis_size("vert")
+    rows = fields * ry * tiles * rz
+    inner, outer = swaps(lax.axis_size("vert"))
+    across = [(0, 1), (1, 0)]
+
+    own = flat(lax.dynamic_index_in_dim(state, span_at, 0, False))
+    away = flat(lax.dynamic_index_in_dim(state, 1 - span_at, 0, False))
+    got = lax.ppermute(away, "span", across)
+    fringe = pl.pallas_call(
+        functools.partial(pack_kernel, (fields, ry, rz, tiles)),
+        out_shape=jax.ShapeDtypeStruct((fields * (ry + 1) * rz, LANES), jnp.float32),
+        name="pack",
+    )(flat(state[0]))
+    in_own = lax.ppermute(own, "vert", inner)
+    out_own = lax.ppermute(own, "vert", outer)
+    fringe = spread(fringe, "case")
+    fringe_got = lax.ppermute(fringe, "span", across)
+    fringe = jnp.concatenate([fringe, fringe_got])
+    in_got = lax.ppermute(got, "vert", inner)
+    out_got = lax.ppermute(got, "vert", outer)
+    fringe_in = lax.ppermute(fringe, "vert", inner)
+    fringe_out = lax.ppermute(fringe, "vert", outer)
+
+    domain = case_at * slots + span_at
+    tx = lax.dynamic_index_in_dim(turbine_x, span_at, 0, False)
+    ty = lax.dynamic_index_in_dim(turbine_y, span_at, 0, False)
+    yaw = lax.dynamic_index_in_dim(yaw_index, span_at, 0, False)
+    z0 = vert_at * rz
+    ints = jnp.stack(
+        [
+            jnp.maximum(HALO - z0, 0),
+            jnp.minimum(HALO + total_z - z0, rz + 2 * HALO),
+            1 - vert_at % 2,
+            HALO + total_z // 2 - z0,
+            span_at * ry,
+        ]
+    ).astype(jnp.int32)
+    ints = jnp.concatenate([ints, tx, ty])
+    angle = (yaw.astype(jnp.float32) - 3.5) * YAW_STEP
+    reals = jnp.stack([jnp.cos(angle), jnp.sin(angle), (domain > 0).astype(jnp.float32)])
+    width = x // 4
+    ramp = 0.5 * (1.0 - jnp.cos(jnp.pi * (jnp.arange(width, dtype=jnp.float32) + 1.0) / width))
+    ramp = jnp.broadcast_to(ramp[None], (8, width))
+
+    smem = pl.BlockSpec(memory_space=pltpu.SMEM)
+    vmem = pl.BlockSpec(memory_space=pltpu.VMEM)
+    ext = rz + 2 * HALO
+    store = 2 * ROW0 + 2 * ry
+    mine, send = pl.pallas_call(
+        functools.partial(main_kernel, (fields, ry, rz, tiles, nt)),
+        out_shape=[jax.ShapeDtypeStruct((rows, LANES), jnp.float32)] * 2,
+        in_specs=[smem, smem] + [vmem] * 10,
+        out_specs=[vmem, vmem],
+        scratch_shapes=[
+            pltpu.VMEM((fields, tiles, ext, store, LANES), jnp.float32),
+            pltpu.VMEM((fields, tiles, ext, store, LANES), jnp.float32),
+            pltpu.VMEM((fields, 2, ext, store, LANES), jnp.float32),
+            pltpu.VMEM((fields, 2, ext, store, LANES), jnp.float32),
+            pltpu.VMEM((ry * rz, LANES), jnp.float32),
+            pltpu.VMEM((2, 2, tiles, 2 * ry // 8, 8, LANES), jnp.float32),
+        ],
+        name="steps",
+    )(ints, reals, own, got, in_own, in_got, out_own, out_got, fringe, fringe_in, fringe_out, ramp)
+    back = lax.ppermute(send, "span", across)
+    out = pl.pallas_call(
+        join_kernel,
+        out_shape=jax.ShapeDtypeStruct((slots, rows, LANES), jnp.float32),
+        in_specs=[smem, vmem, vmem],
+        out_specs=vmem,
+        name="join",
+    )(span_at[None].astype(jnp.int32), mine, back)
+    return unflat(out, fields, ry, rz, x)
 
 
 def extended_2(shard, sides, width):
@@ -100,8 +436,8 @@
     return stencil(fields, extended(fields), weight, cos_yaw, sin_yaw)
 
 
-def make_weight(turbine_x, turbine_y, along_y, along_z, total_y, total_z, active):
-    along_x = jnp.arange(X, dtype=jnp.int32)
+def make_weight(turbine_x, turbine_y, along_y, along_z, total_y, total_z, active, length):
+    along_x = jnp.arange(length, dtype=jnp.int32)
     hit_x = (along_x[None, None, :] == turbine_x[:, :, None]).astype(jnp.float32)
     hit_y = ((along_y[None, None, :] - turbine_y[:, :, None]) % total_y < DISK).astype(jnp.float32)
     plane = jnp.einsum("dky,dkx->dyx", hit_y, hit_x, precision=lax.Precision.HIGHEST)
@@ -114,7 +450,7 @@
     return (jnp.where(keep, earlier[0], later[0]), jnp.maximum(earlier[1], later[1]))
 
 
-def body(state, turbine_x, turbine_y, yaw_index):
+def body_general(state, turbine_x, turbine_y, yaw_index):
     slots = state.shape[0]
     rows_y = state.shape[2]
     rows_z = state.shape[3]
@@ -124,11 +460,11 @@
     active = (domain > 0).astype(jnp.float32)
     along_y = lax.axis_index("span") * rows_y + jnp.arange(rows_y, dtype=jnp.int32)
     along_z = lax.axis_index("vert") * rows_z + jnp.arange(rows_z, dtype=jnp.int32)
-    weight = make_weight(turbine_x, turbine_y, along_y, along_z, total_y, total_z, active)
+    weight = make_weight(turbine_x, turbine_y, along_y, along_z, total_y, total_z, active, state.shape[4])
     angle = (yaw_index.astype(jnp.float32) - 3.5) * YAW_STEP
     cos_yaw = jnp.cos(angle)[:, None, None, None]
     sin_yaw = jnp.sin(angle)[:, None, None, None]
-    width = X // 4
+    width = state.shape[4] // 4
     ramp = 0.5 * (1.0 - jnp.cos(jnp.pi * (jnp.arange(width, dtype=jnp.float32) + 1.0) / width))
     case_at = lax.axis_index("case")
     for step in range(STEPS):
@@ -147,9 +483,17 @@
     return state
 
 
+def body_any(state, turbine_x, turbine_y, yaw_index):
+    slots, _, ry, rz, x = state.shape
+    fits = lax.axis_size("span") == 2 and slots == 2 and lax.axis_size("vert") % 2 == 0
+    fits = fits and ry == 8 and rz % 8 == 0 and x == 4 * LANES
+    chosen = body if fits else body_general
+    return chosen(state, turbine_x, turbine_y, yaw_index)
+
+
 def solution(mesh):
     return jax.shard_map(
-        body,
+        body_any,
         mesh=mesh,
         in_specs=(
             P("case", None, "span", "vert", None),

time: 180 us -> 84.4 us (0.47)
  the two profiles are of different devices: /device:TPU:28 before, /device:TPU:1 now
where the time goes in v1:
time: 84.4 us; the launch traced here: 84.1 us
  Pallas kernels  36.5 us (43%)
  starting transfers between devices  23 us (27%)
  waiting for transfers between devices  14.9 us (18%)
  local copies, waits for them, and re-layouts  6.18 us (7%)
  other arithmetic  2.51 us (3%)
  between operations  1.08 us (1%)
    pallas_call x1, Pallas kernels, body(): pl.pallas_call(functools.partial(main_kernel, (fields, ry, rz, tiles, nt)...  32.2 us
    ppermute x1, waiting for transfers between devices, body(): back = lax.ppermute(send, 'span', across)  7.03 us
    ppermute x2, starting transfers between devices, spread(): moved = lax.ppermute(value, axis, pairs)  6.33 us
    ppermute x1, starting transfers between devices, body(): out_got = lax.ppermute(got, 'vert', outer)  6.24 us
    ppermute x1, waiting for transfers between devices, body(): fringe_out = lax.ppermute(fringe, 'vert', outer)  4.67 us
    ppermute x1, starting transfers between devices, body(): out_own = lax.ppermute(own, 'vert', outer)  4.56 us
    slice x1, local copies, waits for them, and re-layouts, body(): state[0]  2.5 us
    pallas_call x1, Pallas kernels, body(): pl.pallas_call(join_kernel, out_shape=jax.ShapeDtypeStruct((slots, rows,...  2.24 us
  transfers between devices with their start and end apart: 11, of which 4 were waited for; matrix products, arithmetic and copies ran while one was open for 5% of the time, Pallas kernels for 0%

profile of v1, /device:TPU:1, one launch (start us, length us, event | category | flops | bytes accessed | tf_op | source)
XLA Modules:
  0.0 84.1 jit_solution(11743918927885462959)
XLA Ops:
  0.0 2.5 %fusion.2 = (f32[1,4,8,8,512]{4,3,2,1,0:T(8,128)}, f32[1,4,8,8,512]{4,3,2,1,0:T(8,128)S(1)}, f32[1,4,8,8,512]{4,3,2,1,0:T(8,128)S(1)}) fusion(f32[2,4,8,8,512]{4,3,2,1,0:T(8,128)} %param.4, s32[]{:T(128)S(6)} %select_n.42, s32[]{:T(128)S(6)} %select_n.43), kind=kLoop, calls=%fused_computation.11 | loop fusion | bytes 3145736 | tf_op jit(solution)/shard_map/slice | solution.py:292
  2.5 2.0 %pack.1 = f32[288,128]{1,0:T(8,128)} custom-call(f32[1024,128]{1,0:T(8,128)} %bitcast.31), custom_call_target="tpu_custom_call" | custom-call | tf_op jit(solution)/shard_map/pack/pallas_call | solution.py:288
  4.5 5.0 %collective-permute-start.5 = (f32[288,128]{1,0:T(8,128)}, f32[288,128]{1,0:T(8,128)S(1)}, u32[]{:S(2)}, u32[]{:S(2)}) collective-permute-start(f32[288,128]{1,0:T(8,128)} %pack.1), channel_id=1, source_target_pairs={{0,16},{1,17},{2,18},{3,19},{4,20},{5,21},{6,22},{7,23}} | collective-permute-start | bytes 442376 | tf_op jit(solution)/shard_map/ppermute | solution.py:269
  9.5 1.3 %collective-permute-start = (f32[1024,128]{1,0:T(8,128)S(1)}, f32[1024,128]{1,0:T(8,128)S(1)}, u32[]{:S(2)}, u32[]{:S(2)}) collective-permute-start(f32[1024,128]{1,0:T(8,128)S(1)} %bitcast.35), channel_id=1, source_target_pairs={{0,4},{4,0},{1,5},{5,1},{2,6},{6,2},{3,7},{7,3},{8,12},{12,8},{9,1... | collective-permute-start | bytes 1572872 | tf_op jit(solution)/shard_map/ppermute | solution.py:287
  10.8 1.5 %collective-permute-done.5 = f32[288,128]{1,0:T(8,128)S(1)} collective-permute-done((f32[288,128]{1,0:T(8,128)}, f32[288,128]{1,0:T(8,128)S(1)}, u32[]{:S(2)}, u32[]{:S(2)}) %collective-permute-start.5) | collective-permute-done | bytes 147488 | tf_op jit(solution)/shard_map/ppermute | solution.py:269
  12.3 0.9 %broadcast_select_fusion = f32[288,128]{1,0:T(8,128)S(1)} fusion(f32[288,128]{1,0:T(8,128)S(1)} %collective-permute-done.5, f32[288,128]{1,0:T(8,128)} %pack.1, pred[]{:T(512)S(6)} %eq.11), kind=kLoop, calls=%fused_computation.1 | loop fusion | flops 36864 | bytes 442369 | tf_op jit(solution)/shard_map/jit(_where)/select_n | solution.py:270
  13.3 1.3 %collective-permute-start.6 = (f32[288,128]{1,0:T(8,128)S(1)}, f32[288,128]{1,0:T(8,128)S(1)}, u32[]{:S(2)}, u32[]{:S(2)}) collective-permute-start(f32[288,128]{1,0:T(8,128)S(1)} %broadcast_select_fusion), channel_id=1, source_target_pairs={{0,8},{16,24},{1,9},{17,25},{2,10},{18,26},{3,11},{19,27},{4,12},{... | collective-permute-start | bytes 442376 | tf_op jit(solution)/shard_map/ppermute | solution.py:269
  14.6 4.6 %collective-permute-start.3 = (f32[1024,128]{1,0:T(8,128)S(1)}, f32[1024,128]{1,0:T(8,128)S(1)}, u32[]{:S(2)}, u32[]{:S(2)}) collective-permute-start(f32[1024,128]{1,0:T(8,128)S(1)} %bitcast.32), channel_id=1, source_target_pairs={{1,2},{2,1},{5,6},{6,5},{9,10},{10,9},{13,14},{14,13},{17,18},{18,... | collective-permute-start | bytes 1572872 | tf_op jit(solution)/shard_map/ppermute | solution.py:294
  19.2 1.3 %collective-permute-start.7 = (f32[288,128]{1,0:T(8,128)S(1)}, f32[288,128]{1,0:T(8,128)}, u32[]{:S(2)}, u32[]{:S(2)}) collective-permute-start(f32[288,128]{1,0:T(8,128)S(1)} %broadcast_select_fusion.1), channel_id=1, source_target_pairs={{0,4},{4,0},{1,5},{5,1},{2,6},{6,2},{3,7},{7,3},{8,12},{12,8},{9,1... | collective-permute-start | bytes 442376 | tf_op jit(solution)/shard_map/ppermute | solution.py:296
  20.5 1.6 %collective-permute-done.got = f32[1024,128]{1,0:T(8,128)S(1)} collective-permute-done((f32[1024,128]{1,0:T(8,128)S(1)}, f32[1024,128]{1,0:T(8,128)S(1)}, u32[]{:S(2)}, u32[]{:S(2)}) %collective-permute-start) | collective-permute-done | bytes 524320 | tf_op jit(solution)/shard_map/ppermute | solution.py:287
  22.1 6.2 %collective-permute-start.4 = (f32[1024,128]{1,0:T(8,128)S(1)}, f32[1024,128]{1,0:T(8,128)S(1)}, u32[]{:S(2)}, u32[]{:S(2)}) collective-permute-start(f32[1024,128]{1,0:T(8,128)S(1)} %collective-permute-done.got), channel_id=1, source_target_pairs={{1,2},{2,1},{5,6},{6,5},{9,10},{10,9},{13,14},{14,13},{17,18},{18,... | collective-permute-start | bytes 1572872 | tf_op jit(solution)/shard_map/ppermute | solution.py:299
  28.5 0.6 copy-done.10
  29.1 0.7 dynamic_slice.20
  30.7 0.9 %pad_maximum_fusion.p_own = f32[576,128]{1,0:T(8,128)S(1)} fusion(f32[288,128]{1,0:T(8,128)} %collective-permute-done.7, f32[288,128]{1,0:T(8,128)S(1)} %broadcast_select_fusion.1), kind=kLoop, calls=%fused_computation | loop fusion | flops 73728 | bytes 589824 | tf_op jit(solution)/shard_map/concatenate | solution.py:297
  31.6 1.9 %collective-permute-start.9 = (f32[576,128]{1,0:T(8,128)S(1)}, f32[576,128]{1,0:T(8,128)S(1)}, u32[]{:S(2)}, u32[]{:S(2)}) collective-permute-start(f32[576,128]{1,0:T(8,128)S(1)} %pad_maximum_fusion.p_own), channel_id=1, source_target_pairs={{1,2},{2,1},{5,6},{6,5},{9,10},{10,9},{13,14},{14,13},{17,18},{18,... | collective-permute-start | bytes 884744 | tf_op jit(solution)/shard_map/ppermute | solution.py:301
  33.7 0.7 concatenate.6.ints
  34.4 0.6 pad_maximum_fusion.1.reals
  35.0 4.7 %collective-permute-done.9.p_out = f32[576,128]{1,0:T(8,128)S(1)} collective-permute-done((f32[576,128]{1,0:T(8,128)S(1)}, f32[576,128]{1,0:T(8,128)S(1)}, u32[]{:S(2)}, u32[]{:S(2)}) %collective-permute-start.9) | collective-permute-done | bytes 294944 | tf_op jit(solution)/shard_map/ppermute | solution.py:301
  39.7 0.7 broadcast_in_dim.10.ramp_ref
  40.6 32.2 %steps.1 = (f32[1024,128]{1,0:T(8,128)}, f32[1024,128]{1,0:T(8,128)}) custom-call(s32[17]{0:T(128)} %concatenate.6.ints, f32[3]{0:T(128)} %pad_maximum_fusion.1.reals, f32[1024,128]{1,0:T(8,128)} %bitcast.34, f32[1024,128]{1,0:T(8,128)} %copy-done.3, f32[1024,128]{1,0:T(8,128)} %copy-done.5, f32[1024,128]{1,0:T(8,128)} %collective-permute-done.2.in_got, ...), custom_call_target="tpu_custom_call" | custom-call | tf_op jit(solution)/shard_map/steps/pallas_call | solution.py:328
  72.8 1.2 %collective-permute-start.10 = (f32[1024,128]{1,0:T(8,128)}, f32[1024,128]{1,0:T(8,128)S(1)}, u32[]{:S(2)}, u32[]{:S(2)}) collective-permute-start(f32[1024,128]{1,0:T(8,128)} %get-tuple-element.8), channel_id=1, source_target_pairs={{0,4},{4,0},{1,5},{5,1},{2,6},{6,2},{3,7},{7,3},{8,12},{12,8},{9,1... | collective-permute-start | bytes 1572872 | tf_op jit(solution)/shard_map/ppermute | solution.py:343
  74.0 7.0 %collective-permute-done.10.got_ref = f32[1024,128]{1,0:T(8,128)S(1)} collective-permute-done((f32[1024,128]{1,0:T(8,128)}, f32[1024,128]{1,0:T(8,128)S(1)}, u32[]{:S(2)}, u32[]{:S(2)}) %collective-permute-start.10) | collective-permute-done | bytes 524320 | tf_op jit(solution)/shard_map/ppermute | solution.py:343
  81.0 0.8 copy-done.2
  81.9 2.2 %join.1 = f32[2,1024,128]{2,1,0:T(8,128)} custom-call(s32[1]{0:T(128)} %bitcast.ints, f32[1024,128]{1,0:T(8,128)} %get-tuple-element.7.mine_ref, f32[1024,128]{1,0:T(8,128)} %copy-done.2), custom_call_target="tpu_custom_call" | custom-call | tf_op jit(solution)/shard_map/join/pallas_call | solution.py:344
  (33 shorter events, 0.5 us)
Async XLA Ops:
  2.5 18.0 %copy-start = (f32[1,4,8,8,512]{4,3,2,1,0:T(8,128)}, f32[1,4,8,8,512]{4,3,2,1,0:T(8,128)S(1)}, u32[]{:S(2)}) copy-start(f32[1,4,8,8,512]{4,3,2,1,0:T(8,128)S(1)} %get-tuple-element.10) | copy-start | bytes 1572868
  4.5 7.9 %collective-permute-start.5 = (f32[288,128]{1,0:T(8,128)}, f32[288,128]{1,0:T(8,128)S(1)}, u32[]{:S(2)}, u32[]{:S(2)}) collective-permute-start(f32[288,128]{1,0:T(8,128)} %pack.1), channel_id=1, source_target_pairs={{0,16},{1,17},{2,18},{3,19},{4,20},{5,21},{6,22},{7,23}} | collective-permute-start | bytes 442376 | tf_op jit(solution)/shard_map/ppermute | solution.py:269
  9.5 12.6 %collective-permute-start = (f32[1024,128]{1,0:T(8,128)S(1)}, f32[1024,128]{1,0:T(8,128)S(1)}, u32[]{:S(2)}, u32[]{:S(2)}) collective-permute-start(f32[1024,128]{1,0:T(8,128)S(1)} %bitcast.35), channel_id=1, source_target_pairs={{0,4},{4,0},{1,5},{5,1},{2,6},{6,2},{3,7},{7,3},{8,12},{12,8},{9,1... | collective-permute-start | bytes 1572872 | tf_op jit(solution)/shard_map/ppermute | solution.py:287
  13.3 5.9 %collective-permute-start.6 = (f32[288,128]{1,0:T(8,128)S(1)}, f32[288,128]{1,0:T(8,128)S(1)}, u32[]{:S(2)}, u32[]{:S(2)}) collective-permute-start(f32[288,128]{1,0:T(8,128)S(1)} %broadcast_select_fusion), channel_id=1, source_target_pairs={{0,8},{16,24},{1,9},{17,25},{2,10},{18,26},{3,11},{19,27},{4,12},{... | collective-permute-start | bytes 442376 | tf_op jit(solution)/shard_map/ppermute | solution.py:269
  14.6 19.0 %collective-permute-start.3 = (f32[1024,128]{1,0:T(8,128)S(1)}, f32[1024,128]{1,0:T(8,128)S(1)}, u32[]{:S(2)}, u32[]{:S(2)}) collective-permute-start(f32[1024,128]{1,0:T(8,128)S(1)} %bitcast.32), channel_id=1, source_target_pairs={{1,2},{2,1},{5,6},{6,5},{9,10},{10,9},{13,14},{14,13},{17,18},{18,... | collective-permute-start | bytes 1572872 | tf_op jit(solution)/shard_map/ppermute | solution.py:294
  19.2 11.5 %collective-permute-start.7 = (f32[288,128]{1,0:T(8,128)S(1)}, f32[288,128]{1,0:T(8,128)}, u32[]{:S(2)}, u32[]{:S(2)}) collective-permute-start(f32[288,128]{1,0:T(8,128)S(1)} %broadcast_select_fusion.1), channel_id=1, source_target_pairs={{0,4},{4,0},{1,5},{5,1},{2,6},{6,2},{3,7},{7,3},{8,12},{12,8},{9,1... | collective-permute-start | bytes 442376 | tf_op jit(solution)/shard_map/ppermute | solution.py:296
  20.5 14.5 %collective-permute-start.1 = (f32[1024,128]{1,0:T(8,128)S(1)}, f32[1024,128]{1,0:T(8,128)S(1)}, u32[]{:S(2)}, u32[]{:S(2)}) collective-permute-start(f32[1024,128]{1,0:T(8,128)S(1)} %bitcast.33), channel_id=1, source_target_pairs={{0,1},{1,0},{2,3},{3,2},{4,5},{5,4},{6,7},{7,6},{8,9},{9,8},{10,11... | collective-permute-start | bytes 1572872 | tf_op jit(solution)/shard_map/ppermute | solution.py:293
  22.1 18.2 %copy-start.3 = (f32[1024,128]{1,0:T(8,128)}, f32[1024,128]{1,0:T(8,128)S(1)}, u32[]{:S(2)}) copy-start(f32[1024,128]{1,0:T(8,128)S(1)} %collective-permute-done.got) | copy-start | bytes 1572868
  22.1 17.5 %collective-permute-start.4 = (f32[1024,128]{1,0:T(8,128)S(1)}, f32[1024,128]{1,0:T(8,128)S(1)}, u32[]{:S(2)}, u32[]{:S(2)}) collective-permute-start(f32[1024,128]{1,0:T(8,128)S(1)} %collective-permute-done.got), channel_id=1, source_target_pairs={{1,2},{2,1},{5,6},{6,5},{9,10},{10,9},{13,14},{14,13},{17,18},{18,... | collective-permute-start | bytes 1572872 | tf_op jit(solution)/shard_map/ppermute | solution.py:299
  28.4 11.3 %collective-permute-start.2 = (f32[1024,128]{1,0:T(8,128)S(1)}, f32[1024,128]{1,0:T(8,128)}, u32[]{:S(2)}, u32[]{:S(2)}) collective-permute-start(f32[1024,128]{1,0:T(8,128)S(1)} %collective-permute-done.got), channel_id=1, source_target_pairs={{0,1},{1,0},{2,3},{3,2},{4,5},{5,4},{6,7},{7,6},{8,9},{9,8},{10,11... | collective-permute-start | bytes 1572872 | tf_op jit(solution)/shard_map/ppermute | solution.py:298
  28.5 0.7 copy-start.10
  30.6 3.0 %copy-start.8 = (s32[2,6]{1,0:T(2,128)S(1)}, s32[2,6]{1,0:T(2,128)}, u32[]{:S(2)}) copy-start(s32[2,6]{1,0:T(2,128)} %param.5) | copy-start | bytes 148
  30.6 3.0 %copy-start.9 = (s32[2,6]{1,0:T(2,128)S(1)}, s32[2,6]{1,0:T(2,128)}, u32[]{:S(2)}) copy-start(s32[2,6]{1,0:T(2,128)} %param.6) | copy-start | bytes 148
  31.6 8.7 %copy-start.1 = (f32[576,128]{1,0:T(8,128)}, f32[576,128]{1,0:T(8,128)S(1)}, u32[]{:S(2)}) copy-start(f32[576,128]{1,0:T(8,128)S(1)} %pad_maximum_fusion.p_own) | copy-start | bytes 884740
  31.6 8.0 %collective-permute-start.9 = (f32[576,128]{1,0:T(8,128)S(1)}, f32[576,128]{1,0:T(8,128)S(1)}, u32[]{:S(2)}, u32[]{:S(2)}) collective-permute-start(f32[576,128]{1,0:T(8,128)S(1)} %pad_maximum_fusion.p_own), channel_id=1, source_target_pairs={{1,2},{2,1},{5,6},{6,5},{9,10},{10,9},{13,14},{14,13},{17,18},{18,... | collective-permute-start | bytes 884744 | tf_op jit(solution)/shard_map/ppermute | solution.py:301
  33.6 6.8 %copy-start.4 = (f32[1024,128]{1,0:T(8,128)}, f32[1024,128]{1,0:T(8,128)S(1)}, u32[]{:S(2)}) copy-start(f32[1024,128]{1,0:T(8,128)S(1)} %collective-permute-done.3.out_own) | copy-start | bytes 1572868
  33.6 6.1 %collective-permute-start.8 = (f32[576,128]{1,0:T(8,128)S(1)}, f32[576,128]{1,0:T(8,128)}, u32[]{:S(2)}, u32[]{:S(2)}) collective-permute-start(f32[576,128]{1,0:T(8,128)S(1)} %pad_maximum_fusion.p_own), channel_id=1, source_target_pairs={{0,1},{1,0},{2,3},{3,2},{4,5},{5,4},{6,7},{7,6},{8,9},{9,8},{10,11... | collective-permute-start | bytes 884744 | tf_op jit(solution)/shard_map/ppermute | solution.py:300
  35.0 5.4 %copy-start.5 = (f32[1024,128]{1,0:T(8,128)}, f32[1024,128]{1,0:T(8,128)S(1)}, u32[]{:S(2)}) copy-start(f32[1024,128]{1,0:T(8,128)S(1)} %collective-permute-done.1.in_own) | copy-start | bytes 1572868
  39.7 0.7 copy-start.7
  39.7 0.9 %copy-start.6 = (f32[1024,128]{1,0:T(8,128)}, f32[1024,128]{1,0:T(8,128)S(1)}, u32[]{:S(2)}) copy-start(f32[1024,128]{1,0:T(8,128)S(1)} %collective-permute-done.4.out_got) | copy-start | bytes 1572868
  72.8 8.2 %collective-permute-start.10 = (f32[1024,128]{1,0:T(8,128)}, f32[1024,128]{1,0:T(8,128)S(1)}, u32[]{:S(2)}, u32[]{:S(2)}) collective-permute-start(f32[1024,128]{1,0:T(8,128)} %get-tuple-element.8), channel_id=1, source_target_pairs={{0,4},{4,0},{1,5},{5,1},{2,6},{6,2},{3,7},{7,3},{8,12},{12,8},{9,1... | collective-permute-start | bytes 1572872 | tf_op jit(solution)/shard_map/ppermute | solution.py:343
  81.0 0.8 copy-start.2
